TPU v7x, 32 devices: a whole 2x2x4 slice. The times are simulated.
32 devices in a mesh: seg: 8 (over z, x), mp: 4 (over y, core).
Axes of the slice: x: 2, y: 2, z: 4, core: 2. Of those that a mesh axis runs over, the one named last changes fastest.
Arguments:
- patches: bfloat16 [8192, 768], P('seg'), may hold values from -6 to 6
- curve_owner: int32 [8192], P('seg'), may hold values from 0 to 7, as said below
- arrival_slot: int32 [8192], P('seg'), may hold values from 0 to 2047, as said below
- patch_level: int32 [8192], P('seg'), may hold values from 0 to 3
- neighbours: int32 [8192, 16], P('seg'), may hold values from 0 to 8191, as said below
- level_embed: bfloat16 [4, 768], replicated, may hold values from -3 to 3
- norm_gain: float32 [768], replicated, may hold values from 0.5 to 2
- qkv_weight: bfloat16 [768, 3, 768], P(None, None, 'mp')
- out_weight: bfloat16 [768, 768], P('mp'), may hold values from -0.21875 to 0.21875
- cotangent: bfloat16 [8192, 768], P('seg'), may hold values from -6 to 6
Outputs:
- token_grads: float32 [8192, 768], P('seg', 'mp')
- qkv_grad: float32 [768, 3, 768], P(None, None, 'mp')
- out_grad: float32 [768, 768], P('mp')
- gain_grad: float32 [768], P('mp')
Inputs may be any that keep to these rules, and one draw needn't show every extreme that they name: `curve_owner`: every device owns exactly 1024 patches. No device holds more than 256 patches with one owner, and in every draw some device holds exactly 256 patches with some owner. `arrival_slot`: entry d * 1024 + p is s * 256 + k: the patch at position p of owner d is the k-th, counted from 0 in row order, of the rows of device s whose owner is d. The entries of one owner are distinct and name every patch it owns. `neighbours`: row p lists positions within 128 of p on the curve, p itself among them; a position may repeat.
All inputs are finite; a program needn't handle non-finite values.
Results may differ from a plain program's by a relative error of at most 0.029.
Values may be sent and summed in bfloat16 or wider, within the bound.
A program may use at most 64 MiB of HBM per device.

v0:
```python
import jax
import jax.numpy as jnp
from jax import lax
from jax.sharding import PartitionSpec as P

DH = 64
R = 128
EPSILON = 1e-06


def with_halo(cells, sides, width):
    for axis, dim in sides:
        count = lax.axis_size(axis)
        ends = count - 1
        head = lax.slice_in_dim(cells, 0, width, axis=dim)
        tail = lax.slice_in_dim(cells, cells.shape[dim] - width, cells.shape[dim], axis=dim)
        cells = jnp.concatenate(
            [
                lax.ppermute(tail, axis, [(i, (i + 1) % count) for i in range(ends)]),
                cells,
                lax.ppermute(head, axis, [((i + 1) % count, i) for i in range(ends)]),
            ],
            axis=dim,
        )
    return cells


def per_device(
    patches,
    curve_owner,
    arrival_slot,
    patch_level,
    neighbours,
    level_embed,
    norm_gain,
    qkv_weight,
    out_weight,
    cotangent,
):
    segments = lax.axis_size("seg")
    shares = lax.axis_size("mp")
    tok_rows = patches.shape[0]
    model_width = patches.shape[1]
    local_width = qkv_weight.shape[2]
    heads_here = local_width // DH
    capacity = 2 * tok_rows // segments
    share_width = model_width // shares
    first_column = lax.axis_index("mp") * share_width
    onehot = (curve_owner[:, None] == jnp.arange(segments, dtype=jnp.int32)[None, :]).astype(
        jnp.int32
    )
    row_ranks = jnp.sum(onehot * (jnp.cumsum(onehot, axis=0) - onehot), axis=1)
    slot_index = curve_owner * capacity + row_ranks
    columns_here = patches.shape[1]
    buffer = (
        jnp.zeros((segments * capacity, columns_here), patches.dtype).at[slot_index].set(patches)
    )
    arrived = lax.all_to_all(
        buffer.reshape(segments, capacity, columns_here),
        "seg",
        split_axis=0,
        concat_axis=0,
        tiled=True,
    )
    routed = arrived.reshape(segments * capacity, columns_here)[arrival_slot]
    levels_count = level_embed.shape[0]
    level_hot = (patch_level[:, None] == jnp.arange(levels_count, dtype=jnp.int32)[None, :]).astype(
        jnp.bfloat16
    )
    embedded = routed.astype(jnp.float32) + jnp.dot(
        level_hot, level_embed, preferred_element_type=jnp.float32
    )
    inv_rms = lax.rsqrt(jnp.mean(embedded * embedded, axis=1, keepdims=True) + EPSILON)
    normed = embedded * inv_rms
    hidden = (normed * norm_gain).astype(jnp.bfloat16)
    flat_weight = qkv_weight.reshape(model_width, 3 * local_width)
    project = jnp.dot(hidden, flat_weight, preferred_element_type=jnp.float32).astype(jnp.bfloat16)
    queries = project[:, :local_width]
    key_value = project[:, local_width:]
    extended = with_halo(key_value, (("seg", 0),), R)
    grad_out = lax.dot_general(
        cotangent, out_weight, (((1,), (1,)), ((), ())), preferred_element_type=jnp.float32
    ).astype(jnp.bfloat16)
    block_rows = min(tok_rows, 512)
    key_span = block_rows + 2 * R
    score_scale = DH ** (-0.5)
    first_key = lax.axis_index("seg") * tok_rows - R
    grad_ext = jnp.zeros((tok_rows + 2 * R, 2 * local_width), jnp.float32)
    outputs = []
    query_grads = []
    for block_index in range(tok_rows // block_rows):
        block_start = block_index * block_rows
        query_block = queries[block_start : block_start + block_rows].reshape(
            block_rows, heads_here, DH
        )
        pair_block = extended[block_start : block_start + key_span].reshape(
            key_span, 2, heads_here, DH
        )
        key_block = pair_block[:, 0]
        value_block = pair_block[:, 1]
        positions = first_key + block_start + jnp.arange(key_span, dtype=jnp.int32)
        listed = neighbours[block_start : block_start + block_rows]
        allowed = listed[:, 0:1] == positions[None, :]
        for column in range(1, listed.shape[1]):
            allowed = allowed | (listed[:, column : column + 1] == positions[None, :])
        allowed = allowed[None]
        scores = (
            jnp.einsum("qhd,khd->hqk", query_block, key_block, preferred_element_type=jnp.float32)
            * score_scale
        )
        row_top = jnp.max(jnp.where(allowed, scores, -jnp.inf), axis=2, keepdims=True)
        exponent = jnp.where(allowed, jnp.exp(scores - row_top), 0.0)
        probability = exponent / jnp.sum(exponent, axis=2, keepdims=True)
        weights = probability.astype(jnp.bfloat16)
        out_block = jnp.einsum(
            "hqk,khd->qhd", weights, value_block, preferred_element_type=jnp.float32
        ).astype(jnp.bfloat16)
        grad_block = grad_out[block_start : block_start + block_rows].reshape(
            block_rows, heads_here, DH
        )
        row_delta = jnp.sum(
            grad_block.astype(jnp.float32) * out_block.astype(jnp.float32), axis=2
        ).T[:, :, None]
        grad_prob = jnp.einsum(
            "qhd,khd->hqk", grad_block, value_block, preferred_element_type=jnp.float32
        )
        dscore = (probability * (grad_prob - row_delta) * score_scale).astype(jnp.bfloat16)
        dquery = jnp.einsum("hqk,khd->qhd", dscore, key_block, preferred_element_type=jnp.float32)
        grad_key = jnp.einsum(
            "hqk,qhd->khd", dscore, query_block, preferred_element_type=jnp.float32
        )
        dvalue = jnp.einsum("hqk,qhd->khd", weights, grad_block, preferred_element_type=jnp.float32)
        joined = jnp.concatenate(
            [grad_key.reshape(key_span, local_width), dvalue.reshape(key_span, local_width)], axis=1
        )
        grad_ext = grad_ext.at[block_start : block_start + key_span].add(joined)
        outputs.append(out_block.reshape(block_rows, local_width))
        query_grads.append(dquery.reshape(block_rows, local_width))
    rim_rows = jnp.concatenate([grad_ext[:R], grad_ext[tok_rows + R :]], axis=0)
    returned = with_halo(rim_rows, (("seg", 0),), R)
    grad_kv = (
        grad_ext[R : R + tok_rows]
        .at[:R]
        .add(returned[:R])
        .at[tok_rows - R :]
        .add(returned[3 * R :])
    )
    grad_qkv = jnp.concatenate([jnp.concatenate(query_grads, axis=0), grad_kv], axis=1).astype(
        jnp.bfloat16
    )
    attended = jnp.concatenate(outputs, axis=0)
    qkv_part = lax.dot_general(
        hidden, grad_qkv, (((0,), (0,)), ((), ())), preferred_element_type=jnp.float32
    )
    out_part = lax.dot_general(
        attended, cotangent, (((0,), (0,)), ((), ())), preferred_element_type=jnp.float32
    )
    hidden_part = lax.dot_general(
        grad_qkv, flat_weight, (((1,), (1,)), ((), ())), preferred_element_type=jnp.float32
    )
    grad_hidden = lax.psum(hidden_part, "mp")
    scaled = grad_hidden * norm_gain
    full_grads = cotangent.astype(jnp.float32) + inv_rms * (
        scaled - normed * jnp.mean(scaled * normed, axis=1, keepdims=True)
    )
    token_grads = lax.dynamic_slice_in_dim(full_grads, first_column, share_width, 1)
    gain_part = lax.dynamic_slice_in_dim(
        jnp.sum(grad_hidden * normed, axis=0), first_column, share_width, 0
    )
    summed_qkv, summed_out, summed_gain = lax.psum((qkv_part, out_part, gain_part), "seg")
    factor = (tok_rows * segments) ** (-0.5)
    qkv_grad = (summed_qkv * factor).reshape(model_width, 3, local_width)
    return (token_grads, qkv_grad, summed_out * factor, summed_gain * factor)


def solution(mesh):
    placed = (
        P("seg", None),
        P("seg"),
        P("seg"),
        P("seg"),
        P("seg", None),
        P(),
        P(),
        P(None, None, "mp"),
        P("mp", None),
        P("seg", None),
    )
    return jax.shard_map(
        per_device,
        mesh=mesh,
        in_specs=placed,
        out_specs=(P("seg", "mp"), P(None, None, "mp"), P("mp", None), P("mp")),
        check_vma=False,
    )
```

profile of v0, /device:TPU:0, one launch (start us, length us, event | category | flops | bytes accessed | tf_op | source)
XLA Modules:
  0.0 360.0 jit_solution(1146869149718708248)
XLA Ops:
  8.0 2.3 reduce-window.6
  12.2 7.9 %scatter_custom_fusion = bf16[2048,768]{1,0:T(8,128)(2,1)} fusion(s32[1024]{0:T(1024)S(1)} %compare_select_fusion.1, bf16[1024,768]{1,0:T(8,128)(2,1)} %param.18, bf16[]{:T(256)} %constant.136.clone.1), kind=kCustom, calls=%fused_computation.33 | custom fusion | bytes 3146240 | tf_op jit(solution)/shard_map/scatter | solution.py:56
  20.1 7.4 %all-to-all-start = ((bf16[8,256,768]{2,1,0:T(8,128)(2,1)}), bf16[8,256,768]{2,1,0:T(8,128)(2,1)}, u32[]{:S(2)}, u32[]{:S(2)}) async-start(bf16[8,256,768]{2,1,0:T(8,128)(2,1)} %bitcast.153), calls=%async_computation | async-start | bytes 6291456 | tf_op jit(solution)/shard_map/all_to_all | solution.py:58
  29.1 4.8 %compare_or_fusion = pred[512,768]{1,0:T(8,128)(4,1)} fusion(s32[768]{0:T(1024)S(1)} %iota_add_fusion, s32[512]{0:T(512)S(1)} %bitcast.222, s32[512]{0:T(512)S(1)} %bitcast.221, s32[512]{0:T(512)S(1)} %bitcast.197, s32[512]{0:T(512)S(1)} %bitcast.198, s32[512]{0:T(512)S(1)} %bitcast.199, s32[512]{0:T(512)S(1)} %bitcast.200, s32[512]{0:T(512)S(1)} %bitcast.201, ...), kind=kLoop, calls=%fused_computation.35 | loop fusion | flops 12189696 | bytes 429056 | tf_op jit(solution)/shard_map/or | solution.py:105
  33.9 4.8 %compare_or_fusion.1 = pred[512,768]{1,0:T(8,128)(4,1)} fusion(s32[768]{0:T(1024)S(1)} %iota_add_fusion.1, s32[512]{0:T(512)S(1)} %bitcast.191, s32[512]{0:T(512)S(1)} %bitcast.192, s32[512]{0:T(512)S(1)} %bitcast.193, s32[512]{0:T(512)S(1)} %bitcast.194, s32[512]{0:T(512)S(1)} %bitcast.195, s32[512]{0:T(512)S(1)} %bitcast.210, s32[512]{0:T(512)S(1)} %bitcast.211, ...), kind=kLoop, calls=%fused_computation.36 | loop fusion | flops 12189696 | bytes 429056 | tf_op jit(solution)/shard_map/or | solution.py:105
  38.6 59.7 %all-to-all-done = bf16[8,256,768]{2,1,0:T(8,128)(2,1)} async-done(((bf16[8,256,768]{2,1,0:T(8,128)(2,1)}), bf16[8,256,768]{2,1,0:T(8,128)(2,1)}, u32[]{:S(2)}, u32[]{:S(2)}) %all-to-all-start) | async-done | bytes 3145760 | tf_op jit(solution)/shard_map/all_to_all | solution.py:58
  98.3 7.9 %gather_fusion = bf16[1024,768]{1,0:T(8,128)(2,1)} fusion(bf16[2048,768]{1,0:T(8,128)(2,1)} %bitcast.3, s32[1024]{0:T(1024)S(1)} %fusion.43), kind=kCustom, calls=%fused_computation | custom fusion | bytes 3149824 | tf_op jit(solution)/shard_map/gather | solution.py:65
  106.2 1.7 copy.18
  107.9 1.3 multiply_reduce_fusion.2
  111.7 1.3 collective-permute-start.1
  113.0 4.7 %collective-permute-start = (bf16[128,384]{0,1:T(8,128)(2,1)S(1)}, bf16[128,384]{0,1:T(8,128)(2,1)S(1)}, u32[]{:S(2)}, u32[]{:S(2)}) collective-permute-start(bf16[128,384]{0,1:T(8,128)(2,1)S(1)} %get-tuple-element.62), channel_id=1, source_target_pairs={{0,4},{4,8},{8,12},{12,16},{16,20},{20,24},{24,28},{1,5},{5,9},{9,... | collective-permute-start | bytes 294920 | tf_op jit(solution)/shard_map/ppermute | solution.py:19
  119.9 5.7 %fusion.57 = (f32[3,512]{1,0:T(4,128)S(1)}, f32[3,512,768]{2,1,0:T(8,128)}) fusion(pred[512,768]{1,0:T(8,128)(4,1)} %compare_or_fusion.1, bf16[512,3,64]{0,2,1:T(8,128)(2,1)S(1)} %bitcast.181, bf16[768,2,3,64]{0,3,2,1:T(8,128)(2,1)S(1)} %bitcast.164), kind=kOutput, calls=%fused_computation.108 | convolution fusion | flops 309068544 | bytes 6494208 | tf_op jit(solution)/shard_map/sub | solution.py:112
  125.6 2.7 fusion.17
  128.3 1.5 multiply_reduce_fusion.4
  129.8 1.3 fusion.60
  131.2 5.7 %fusion.58 = (f32[3,512]{1,0:T(4,128)S(1)}, f32[3,512,768]{2,1,0:T(8,128)}) fusion(pred[512,768]{1,0:T(8,128)(4,1)} %compare_or_fusion, bf16[512,3,64]{0,2,1:T(8,128)(2,1)} %bitcast.179, bf16[768,2,3,64]{0,3,2,1:T(8,128)(2,1)S(1)} %bitcast.160), kind=kOutput, calls=%fused_computation.109 | convolution fusion | flops 309068544 | bytes 6494208 | tf_op jit(solution)/shard_map/sub | solution.py:112
  136.9 2.8 fusion.18
  139.8 1.5 multiply_reduce_fusion.3
  144.2 1.4 multiply_convert_fusion
  147.2 4.3 %collective-permute-start.2 = (f32[128,384]{0,1:T(8,128)S(1)}, f32[128,384]{0,1:T(8,128)S(1)}, u32[]{:S(2)}, u32[]{:S(2)}) collective-permute-start(f32[128,384]{0,1:T(8,128)S(1)} %slice.336), channel_id=1, source_target_pairs={{0,4},{4,8},{8,12},{12,16},{16,20},{20,24},{24,28},{1,5},{5,9},{9,... | collective-permute-start | bytes 589832 | tf_op jit(solution)/shard_map/ppermute | solution.py:19
  152.6 2.1 collective-permute-done.2
  154.7 1.4 collective-permute-start.3
  157.0 6.7 %collective-permute-done.3 = f32[128,384]{0,1:T(8,128)S(1)} collective-permute-done((f32[128,384]{0,1:T(8,128)S(1)}, f32[128,384]{0,1:T(8,128)S(1)}, u32[]{:S(2)}, u32[]{:S(2)}) %collective-permute-start.3) | collective-permute-done | bytes 196640 | tf_op jit(solution)/shard_map/ppermute | solution.py:21
  163.8 3.1 fusion.29
  168.0 1.3 fusion.30
  169.3 4.3 %fusion.28 = f32[768,576]{0,1:T(8,128)} fusion(bf16[1024,384]{0,1:T(8,128)(2,1)S(1)} %convert.16, bf16[512,192]{0,1:T(8,128)(2,1)S(1)} %bitcast.186, bf16[512,192]{0,1:T(8,128)(2,1)S(1)} %bitcast.184, f32[1024,768]{0,1:T(8,128)} %copy-done.1, f32[768]{0:T(1024)S(1)} %copy-done.13), kind=kOutput, calls=%fused_computation.56 | convolution fusion | flops 911081472 | bytes 6097920 | tf_op jit(solution)/shard_map/dot_general | solution.py:152
  174.0 62.2 %all-reduce.5.cloned.1.call-done = f32[1024,768]{0,1:T(8,128)} async-done(((f32[1024,768]{0,1:T(8,128)}), f32[1024,768]{0,1:T(8,128)}) %all-reduce.5.cloned.1.call-update) | async-done | bytes 3145744 | tf_op jit(solution)/shard_map/psum | solution.py:161
  236.2 5.2 %multiply_reduce_fusion = (f32[768]{0:T(1024)S(1)}, f32[1024]{0:T(1024)S(1)}, f32[1024,768]{0,1:T(8,128)}) fusion(f32[1024,768]{0,1:T(8,128)} %all-reduce.5.cloned.1.call-done, f32[1024,768]{0,1:T(8,128)} %copy-done.1, f32[768]{0:T(1024)S(1)} %copy-done.13), kind=kLoop, calls=%fused_computation.14 | loop fusion | flops 3930368 | bytes 9447424 | tf_op jit(solution)/shard_map/reduce_sum | solution.py:168
  241.5 22.3 %psum.31 = f32[192]{0:T(256)S(1)} all-reduce(f32[192]{0:T(256)S(1)} %dynamic_slice.7), channel_id=1, replica_groups=mesh['seg'=8,'mp'=4] {'seg'}, use_global_device_ids=true, to_apply=%region_16.17 | all-reduce | flops 192 | bytes 1536 | tf_op jit(solution)/shard_map/psum | solution.py:170
  264.4 2.5 fusion.22
  266.9 82.6 %all-reduce.7.cloned.1.call-done = (f32[768,576]{0,1:T(8,128)}, f32[192,768]{1,0:T(8,128)}) async-done(((f32[768,576]{0,1:T(8,128)}, f32[192,768]{1,0:T(8,128)}), (f32[768,576]{0,1:T(8,128)}, f32[192,768]{1,0:T(8,128)})) %all-reduce.7.cloned.1.call-update) | async-done | bytes 2359312 | tf_op jit(solution)/shard_map/psum | solution.py:170
  349.4 2.9 broadcast_multiply_fusion.1
  (93 shorter events, 18.2 us)
Async XLA Ops:
  7.2 20.5 %copy-start = (bf16[1024,768]{1,0:T(8,128)(2,1)S(1)}, bf16[1024,768]{1,0:T(8,128)(2,1)}, u32[]{:S(2)}) copy-start(bf16[1024,768]{1,0:T(8,128)(2,1)} %param.27) | copy-start | bytes 4718596
  20.1 7.5 %copy-start.15 = (s32[1024]{0:T(1024)S(1)}, s32[1024]{0:T(1024)}, u32[]{:S(2)}) copy-start(s32[1024]{0:T(1024)} %param.20) | copy-start | bytes 12292
  20.1 7.5 %copy-start.11 = (s32[1024,16]{0,1:T(8,128)S(1)}, s32[1024,16]{0,1:T(8,128)}, u32[]{:S(2)}) copy-start(s32[1024,16]{0,1:T(8,128)} %param.22) | copy-start | bytes 196612
  20.1 7.6 %copy-start.18 = (bf16[192,768]{1,0:T(8,128)(2,1)S(1)}, bf16[192,768]{1,0:T(8,128)(2,1)}, u32[]{:S(2)}) copy-start(bf16[192,768]{1,0:T(8,128)(2,1)} %param.26) | copy-start | bytes 884740
  20.1 78.2 %all-to-all-start = ((bf16[8,256,768]{2,1,0:T(8,128)(2,1)}), bf16[8,256,768]{2,1,0:T(8,128)(2,1)}, u32[]{:S(2)}, u32[]{:S(2)}) async-start(bf16[8,256,768]{2,1,0:T(8,128)(2,1)} %bitcast.153), calls=%async_computation | async-start | bytes 6291456 | tf_op jit(solution)/shard_map/all_to_all | solution.py:58
  27.5 208.7 %all-reduce.5.cloned.1.call-start = ((), (), s32[]{:S(2)}) async-start(), calls=%async_computation.1 | async-start | bytes 6291456 | tf_op jit(solution)/shard_map/psum | solution.py:161
  106.2 1.8 copy-start.12
  106.2 1.8 copy-start.14
  109.3 0.8 copy-start.13
  109.3 1.2 copy-start.16
  110.1 1.6 copy-start.1
  111.7 6.8 %collective-permute-start.1 = (bf16[128,384]{0,1:T(8,128)(2,1)S(1)}, bf16[128,384]{0,1:T(8,128)(2,1)S(1)}, u32[]{:S(2)}, u32[]{:S(2)}) collective-permute-start(bf16[128,384]{0,1:T(8,128)(2,1)S(1)} %get-tuple-element.61), channel_id=1, source_target_pairs={{4,0},{8,4},{12,8},{16,12},{20,16},{24,20},{28,24},{5,1},{9,5},{13... | collective-permute-start | bytes 294920 | tf_op jit(solution)/shard_map/ppermute | solution.py:21
  113.0 6.8 %collective-permute-start = (bf16[128,384]{0,1:T(8,128)(2,1)S(1)}, bf16[128,384]{0,1:T(8,128)(2,1)S(1)}, u32[]{:S(2)}, u32[]{:S(2)}) collective-permute-start(bf16[128,384]{0,1:T(8,128)(2,1)S(1)} %get-tuple-element.62), channel_id=1, source_target_pairs={{0,4},{4,8},{8,12},{12,16},{16,20},{20,24},{24,28},{1,5},{5,9},{9,... | collective-permute-start | bytes 294920 | tf_op jit(solution)/shard_map/ppermute | solution.py:19
  118.5 7.1 %copy-start.8 = (bf16[512,192]{0,1:T(8,128)(2,1)}, bf16[512,192]{0,1:T(8,128)(2,1)S(1)}, u32[]{:S(2)}) copy-start(bf16[512,192]{0,1:T(8,128)(2,1)S(1)} %get-tuple-element.64) | copy-start | bytes 589828
  125.6 2.7 copy-start.3
  131.2 10.6 %slice-start = ((s8[4718592]{0:T(1024)(128)(4,1)}), s8[524288]{0:T(1024)(128)(4,1)S(1)}, s32[]{:S(2)}) async-start(s8[4718592]{0:T(1024)(128)(4,1)} %bitcast.154), calls=%async_computation.3 | async-start | bytes 1048576
  136.9 4.9 %slice-start.1 = ((s8[4718592]{0:T(1024)(128)(4,1)}), s8[4194304]{0:T(1024)(128)(4,1)S(1)}, s32[]{:S(2)}) async-start(s8[4718592]{0:T(1024)(128)(4,1)} %bitcast.154), calls=%async_computation.4 | async-start | bytes 8388608
  139.8 2.1 copy-start.4
  141.3 2.4 slice-start.2
  141.8 1.3 copy-start.9
  141.9 2.3 slice-start.3
  144.2 1.4 copy-start.7
  145.5 1.1 copy-start.2
  147.2 7.5 %collective-permute-start.2 = (f32[128,384]{0,1:T(8,128)S(1)}, f32[128,384]{0,1:T(8,128)S(1)}, u32[]{:S(2)}, u32[]{:S(2)}) collective-permute-start(f32[128,384]{0,1:T(8,128)S(1)} %slice.336), channel_id=1, source_target_pairs={{0,4},{4,8},{8,12},{12,16},{16,20},{20,24},{24,28},{1,5},{5,9},{9,... | collective-permute-start | bytes 589832 | tf_op jit(solution)/shard_map/ppermute | solution.py:19
  154.7 9.1 %copy-start.17 = (bf16[768,3,192]{0,2,1:T(8,128)(2,1)S(1)}, bf16[768,3,192]{0,2,1:T(8,128)(2,1)}, u32[]{:S(2)}) copy-start(bf16[768,3,192]{0,2,1:T(8,128)(2,1)} %param.25) | copy-start | bytes 2654212
  154.7 8.9 %collective-permute-start.3 = (f32[128,384]{0,1:T(8,128)S(1)}, f32[128,384]{0,1:T(8,128)S(1)}, u32[]{:S(2)}, u32[]{:S(2)}) collective-permute-start(f32[128,384]{0,1:T(8,128)S(1)} %get-tuple-element.59), channel_id=1, source_target_pairs={{4,0},{8,4},{12,8},{16,12},{20,16},{24,20},{28,24},{5,1},{9,5},{13... | collective-permute-start | bytes 589832 | tf_op jit(solution)/shard_map/ppermute | solution.py:21
  167.0 0.9 copy-start.5
  167.0 1.0 copy-start.6
  167.0 182.4 %all-reduce.7.cloned.1.call-start = ((), (), s32[]{:S(2)}) async-start(), calls=%async_computation.2 | async-start | bytes 4718592 | tf_op jit(solution)/shard_map/psum | solution.py:170
  349.4 2.9 copy-start.10
Sparse Core Ops, SparseCore 0:
  167.1 69.0 all-reduce.4
  240.4 108.9 all-reduce.6
where the time goes:
time: 361 us; the launch traced here: 360 us
  waiting for transfers between devices  215 us (60%)
  other arithmetic  33.5 us (9%)
  matrix products  33.5 us (9%)
  local copies, waits for them, and re-layouts  22.3 us (6%)
  blocking collectives  22.3 us (6%)
  starting transfers between devices  19.5 us (5%)
  between operations  14.5 us (4%)
    psum x1, waiting for transfers between devices, per_device(): lax.psum((qkv_part, out_part, gain_part), 'seg')  82.6 us
    psum x1, waiting for transfers between devices, per_device(): grad_hidden = lax.psum(hidden_part, 'mp')  62.2 us
    all_to_all x1, waiting for transfers between devices, per_device(): lax.all_to_all(buffer.reshape(segments, capacity, columns_here), 'seg', s...  59.7 us
    psum x1, blocking collectives, per_device(): lax.psum((qkv_part, out_part, gain_part), 'seg')  22.3 us
    sub x2, matrix products, per_device(): exponent = jnp.where(allowed, jnp.exp(scores - row_top), 0.0)  11.4 us
    gather x2, local copies, waits for them, and re-layouts, per_device(): routed = arrived.reshape(segments * capacity, columns_here)[arrival_slot]  9.59 us
    or x2, other arithmetic, per_device(): allowed = allowed | (listed[:, column:column + 1] == positions[None, :])  9.56 us
    ppermute x2, starting transfers between devices, with_halo(): lax.ppermute(tail, axis, [(i, (i + 1) % count) for i in range(ends)])  9.05 us
  transfers between devices with their start and end apart: 7, of which 6 were waited for; matrix products, arithmetic and copies ran while one was open for 8% of the time, Pallas kernels for 0%

commit v1 on v0

--- a/solution.py
+++ b/solution.py
@@ -6,6 +6,12 @@
 DH = 64
 R = 128
 EPSILON = 1e-06
+
+
+def gather_and_add(x, name):
+    shards = lax.all_gather(x, name, axis=0, tiled=False)
+    summed = shards.sum(axis=0)
+    return summed
 
 
 def with_halo(cells, sides, width):
@@ -158,7 +164,7 @@
     hidden_part = lax.dot_general(
         grad_qkv, flat_weight, (((1,), (1,)), ((), ())), preferred_element_type=jnp.float32
     )
-    grad_hidden = lax.psum(hidden_part, "mp")
+    grad_hidden = gather_and_add(hidden_part, "mp")
     scaled = grad_hidden * norm_gain
     full_grads = cotangent.astype(jnp.float32) + inv_rms * (
         scaled - normed * jnp.mean(scaled * normed, axis=1, keepdims=True)

time: 361 us -> 327 us (0.906)
  waiting for transfers between devices: 215 us -> 173 us
  other arithmetic: 33.5 us -> 41.7 us
    psum x1 -> x0, waiting for transfers between devices: 62.2 us -> none  [per_device(): grad_hidden = lax.psum(hidden_part, 'mp')]
    psum x1, waiting for transfers between devices: 82.6 us -> 104 us  [per_device(): lax.psum((qkv_part, out_part, gain_part), 'seg')]
    reduce_sum x0 -> x1, other arithmetic: none -> 7.43 us  [gather_and_add(): summed = shards.sum(axis=0)]
  transfers between devices with their start and end apart: 7 -> 7, of which waited for: 6 -> 5; matrix products, arithmetic and copies ran while one was open for 8% -> 7% of each run, Pallas kernels for 0% -> 0%
where the time goes in v1:
time: 327 us
  waiting for transfers between devices  173 us (53%)
  other arithmetic  41.7 us (13%)
  matrix products  30.8 us (9%)
  local copies, waits for them, and re-layouts  25.7 us (8%)
  starting transfers between devices  19.6 us (6%)
  blocking collectives  19.6 us (6%)
  between operations  16 us (5%)
    psum x1, waiting for transfers between devices, per_device(): lax.psum((qkv_part, out_part, gain_part), 'seg')  104 us
    all_to_all x1, waiting for transfers between devices, per_device(): lax.all_to_all(buffer.reshape(segments, capacity, columns_here), 'seg', s...  59.7 us
    psum x1, blocking collectives, per_device(): lax.psum((qkv_part, out_part, gain_part), 'seg')  19.6 us
    sub x2, matrix products, per_device(): exponent = jnp.where(allowed, jnp.exp(scores - row_top), 0.0)  10.8 us
    gather x2, local copies, waits for them, and re-layouts, per_device(): routed = arrived.reshape(segments * capacity, columns_here)[arrival_slot]  9.59 us
    or x2, other arithmetic, per_device(): allowed = allowed | (listed[:, column:column + 1] == positions[None, :])  9.56 us
    ppermute x2, starting transfers between devices, with_halo(): lax.ppermute(tail, axis, [(i, (i + 1) % count) for i in range(ends)])  9.19 us
    scatter x1, local copies, waits for them, and re-layouts, per_device(): jnp.zeros((segments * capacity, columns_here), patches.dtype).at[slot_index]  7.9 us
  transfers between devices with their start and end apart: 7, of which 5 were waited for; matrix products, arithmetic and copies ran while one was open for 7% of the time, Pallas kernels for 0%

profile of v1, /device:TPU:0, one launch (start us, length us, event | category | flops | bytes accessed | tf_op | source)
XLA Modules:
  0.0 326.7 jit_solution(14377422828461093244)
XLA Ops:
  8.8 2.3 reduce-window.6
  13.0 7.9 %scatter_custom_fusion = bf16[2048,768]{1,0:T(8,128)(2,1)} fusion(s32[1024]{0:T(1024)S(1)} %compare_select_fusion.1, bf16[1024,768]{1,0:T(8,128)(2,1)} %param.18, bf16[]{:T(256)} %constant.136.clone.1), kind=kCustom, calls=%fused_computation.33 | custom fusion | bytes 3146240 | tf_op jit(solution)/shard_map/scatter | solution.py:62
  20.9 7.4 %all-to-all-start = ((bf16[8,256,768]{2,1,0:T(8,128)(2,1)}), bf16[8,256,768]{2,1,0:T(8,128)(2,1)}, u32[]{:S(2)}, u32[]{:S(2)}) async-start(bf16[8,256,768]{2,1,0:T(8,128)(2,1)} %bitcast.154), calls=%async_computation | async-start | bytes 6291456 | tf_op jit(solution)/shard_map/all_to_all | solution.py:64
  29.9 4.8 %compare_or_fusion.1 = pred[512,768]{1,0:T(8,128)(4,1)} fusion(s32[768]{0:T(1024)S(1)} %iota_add_fusion.1, s32[512]{0:T(512)S(1)} %bitcast.204, s32[512]{0:T(512)S(1)} %bitcast.205, s32[512]{0:T(512)S(1)} %bitcast.206, s32[512]{0:T(512)S(1)} %bitcast.207, s32[512]{0:T(512)S(1)} %bitcast.208, s32[512]{0:T(512)S(1)} %bitcast.211, s32[512]{0:T(512)S(1)} %bitcast.212, ...), kind=kLoop, calls=%fused_computation.36 | loop fusion | flops 12189696 | bytes 429056 | tf_op jit(solution)/shard_map/or | solution.py:111
  34.7 4.8 %compare_or_fusion = pred[512,768]{1,0:T(8,128)(4,1)} fusion(s32[768]{0:T(1024)S(1)} %iota_add_fusion, s32[512]{0:T(512)S(1)} %bitcast.210, s32[512]{0:T(512)S(1)} %bitcast.209, s32[512]{0:T(512)S(1)} %bitcast.191, s32[512]{0:T(512)S(1)} %bitcast.192, s32[512]{0:T(512)S(1)} %bitcast.193, s32[512]{0:T(512)S(1)} %bitcast.194, s32[512]{0:T(512)S(1)} %bitcast.195, ...), kind=kLoop, calls=%fused_computation.35 | loop fusion | flops 12189696 | bytes 429056 | tf_op jit(solution)/shard_map/or | solution.py:111
  39.5 59.7 %all-to-all-done = bf16[8,256,768]{2,1,0:T(8,128)(2,1)} async-done(((bf16[8,256,768]{2,1,0:T(8,128)(2,1)}), bf16[8,256,768]{2,1,0:T(8,128)(2,1)}, u32[]{:S(2)}, u32[]{:S(2)}) %all-to-all-start) | async-done | bytes 3145760 | tf_op jit(solution)/shard_map/all_to_all | solution.py:64
  99.1 7.9 %gather_fusion = bf16[1024,768]{1,0:T(8,128)(2,1)} fusion(bf16[2048,768]{1,0:T(8,128)(2,1)} %bitcast.3, s32[1024]{0:T(1024)S(1)} %fusion.43), kind=kCustom, calls=%fused_computation | custom fusion | bytes 3149824 | tf_op jit(solution)/shard_map/gather | solution.py:71
  107.0 1.7 copy.19
  108.8 1.3 multiply_reduce_fusion.2
  112.6 1.4 collective-permute-start.1
  114.0 4.7 %collective-permute-start = (bf16[128,384]{0,1:T(8,128)(2,1)S(1)}, bf16[128,384]{0,1:T(8,128)(2,1)S(1)}, u32[]{:S(2)}, u32[]{:S(2)}) collective-permute-start(bf16[128,384]{0,1:T(8,128)(2,1)S(1)} %get-tuple-element.62), channel_id=1, source_target_pairs={{0,4},{4,8},{8,12},{12,16},{16,20},{20,24},{24,28},{1,5},{5,9},{9,... | collective-permute-start | bytes 294920 | tf_op jit(solution)/shard_map/ppermute | solution.py:25
  120.9 4.4 %fusion.57 = (f32[3,512]{1,0:T(4,128)S(1)}, f32[3,512,768]{2,1,0:T(8,128)}) fusion(pred[512,768]{1,0:T(8,128)(4,1)S(1)} %copy-done.9, bf16[512,3,64]{0,2,1:T(8,128)(2,1)S(1)} %bitcast.178, bf16[768,2,3,64]{0,3,2,1:T(8,128)(2,1)S(1)} %bitcast.159), kind=kOutput, calls=%fused_computation.108 | convolution fusion | flops 309068544 | bytes 6494208 | tf_op jit(solution)/shard_map/sub | solution.py:118
  125.3 2.7 fusion.17
  128.6 1.5 multiply_reduce_fusion.4
  130.1 6.4 %fusion.58 = (f32[3,512]{1,0:T(4,128)}, f32[3,512,768]{2,1,0:T(8,128)}) fusion(pred[512,768]{1,0:T(8,128)(4,1)} %compare_or_fusion, bf16[512,3,64]{0,2,1:T(8,128)(2,1)} %bitcast.180, bf16[768,2,3,64]{0,3,2,1:T(8,128)(2,1)S(1)} %bitcast.163), kind=kOutput, calls=%fused_computation.109 | convolution fusion | flops 309068544 | bytes 6494208 | tf_op jit(solution)/shard_map/sub | solution.py:118
  136.5 2.7 fusion.18
  141.6 1.4 multiply_convert_fusion
  144.4 1.4 multiply_convert_fusion.1
  147.1 4.5 %collective-permute-start.2 = (f32[128,384]{0,1:T(8,128)S(1)}, f32[128,384]{0,1:T(8,128)S(1)}, u32[]{:S(2)}, u32[]{:S(2)}) collective-permute-start(f32[128,384]{0,1:T(8,128)S(1)} %slice.336), channel_id=1, source_target_pairs={{0,4},{4,8},{8,12},{12,16},{16,20},{20,24},{24,28},{1,5},{5,9},{9,... | collective-permute-start | bytes 589832 | tf_op jit(solution)/shard_map/ppermute | solution.py:25
  152.4 2.3 collective-permute-done.2
  156.1 1.3 fusion.30
  157.4 6.2 %collective-permute-done.3 = f32[128,384]{0,1:T(8,128)S(1)} collective-permute-done((f32[128,384]{0,1:T(8,128)S(1)}, f32[128,384]{0,1:T(8,128)S(1)}, u32[]{:S(2)}, u32[]{:S(2)}) %collective-permute-start.3) | collective-permute-done | bytes 196640 | tf_op jit(solution)/shard_map/ppermute | solution.py:27
  163.8 2.4 fusion.28
  167.1 4.2 %fusion.29 = f32[1024,768]{1,0:T(8,128)} fusion(bf16[768,576]{0,1:T(8,128)(2,1)} %bitcast.222, bf16[1024,384]{0,1:T(8,128)(2,1)S(1)} %convert.16, bf16[512,192]{0,1:T(8,128)(2,1)S(1)} %bitcast.183, bf16[512,192]{0,1:T(8,128)(2,1)S(1)} %bitcast.185), kind=kOutput, calls=%fused_computation.57 | convolution fusion | flops 909508608 | bytes 5210112 | tf_op jit(solution)/shard_map/dot_general | solution.py:164
  171.8 103.8 %all-reduce.4.cloned.1.call-done = (f32[768,576]{0,1:T(8,128)}, f32[192,768]{1,0:T(8,128)}) async-done(((f32[768,576]{0,1:T(8,128)}, f32[192,768]{1,0:T(8,128)}), (f32[768,576]{0,1:T(8,128)}, f32[192,768]{1,0:T(8,128)})) %all-reduce.4.cloned.1.call-update) | async-done | bytes 2359312 | tf_op jit(solution)/shard_map/psum | solution.py:176
  275.7 1.9 broadcast_multiply_fusion.2
  277.6 2.8 broadcast_multiply_fusion.1
  280.4 7.4 %reduce_sum.87 = f32[1024,768]{1,0:T(8,128)} reduce(f32[4,1024,768]{2,1,0:T(8,128)} %bitcast.153, f32[]{:T(128)} %constant.140.clone.1), dimensions={0}, to_apply=%region_11.12 | reduce | flops 2359296 | bytes 15728644 | tf_op jit(solution)/shard_map/reduce_sum | solution.py:13
  287.9 3.5 %copy.20 = f32[1024,768]{0,1:T(8,128)} copy(f32[1024,768]{1,0:T(8,128)} %reduce_sum.87) | data formatting | bytes 6291456 | tf_op jit(solution)/shard_map/reduce_sum | solution.py:13
  291.4 5.2 %multiply_reduce_fusion = (f32[768]{0:T(1024)S(1)}, f32[1024]{0:T(1024)S(1)}, f32[1024,768]{0,1:T(8,128)}) fusion(f32[1024,768]{0,1:T(8,128)} %copy.20, f32[1024,768]{0,1:T(8,128)} %copy-done.1, f32[768]{0:T(1024)S(1)} %copy-done.17), kind=kLoop, calls=%fused_computation.14 | loop fusion | flops 3930368 | bytes 9447424 | tf_op jit(solution)/shard_map/reduce_sum | solution.py:174
  296.6 19.6 %psum.23 = f32[192]{0:T(256)S(1)} all-reduce(f32[192]{0:T(256)S(1)} %dynamic_slice.7), channel_id=1, replica_groups=mesh['seg'=8,'mp'=4] {'seg'}, use_global_device_ids=true, to_apply=%region_16.17 | all-reduce | flops 192 | bytes 1536 | tf_op jit(solution)/shard_map/psum | solution.py:176
  316.8 2.5 fusion.22
  (96 shorter events, 18.6 us)
Async XLA Ops:
  8.0 20.5 %copy-start = (bf16[1024,768]{1,0:T(8,128)(2,1)S(1)}, bf16[1024,768]{1,0:T(8,128)(2,1)}, u32[]{:S(2)}) copy-start(bf16[1024,768]{1,0:T(8,128)(2,1)} %param.27) | copy-start | bytes 4718596
  20.9 7.5 %copy-start.19 = (s32[1024]{0:T(1024)S(1)}, s32[1024]{0:T(1024)}, u32[]{:S(2)}) copy-start(s32[1024]{0:T(1024)} %param.20) | copy-start | bytes 12292
  20.9 7.5 %copy-start.12 = (s32[1024,16]{0,1:T(8,128)S(1)}, s32[1024,16]{0,1:T(8,128)}, u32[]{:S(2)}) copy-start(s32[1024,16]{0,1:T(8,128)} %param.22) | copy-start | bytes 196612
  20.9 7.6 %copy-start.21 = (bf16[192,768]{1,0:T(8,128)(2,1)S(1)}, bf16[192,768]{1,0:T(8,128)(2,1)}, u32[]{:S(2)}) copy-start(bf16[192,768]{1,0:T(8,128)(2,1)} %param.26) | copy-start | bytes 884740
  20.9 78.2 %all-to-all-start = ((bf16[8,256,768]{2,1,0:T(8,128)(2,1)}), bf16[8,256,768]{2,1,0:T(8,128)(2,1)}, u32[]{:S(2)}, u32[]{:S(2)}) async-start(bf16[8,256,768]{2,1,0:T(8,128)(2,1)} %bitcast.154), calls=%async_computation | async-start | bytes 6291456 | tf_op jit(solution)/shard_map/all_to_all | solution.py:64
  28.3 247.3 %all-reduce.4.cloned.1.call-start = ((), (), s32[]{:S(2)}) async-start(), calls=%async_computation.2 | async-start | bytes 4718592 | tf_op jit(solution)/shard_map/psum | solution.py:176
  107.0 1.8 copy-start.16
  107.0 1.8 copy-start.18
  110.1 0.8 copy-start.17
  110.1 1.2 copy-start.20
  110.9 1.6 copy-start.1
  112.6 8.3 %copy-start.9 = (pred[512,768]{1,0:T(8,128)(4,1)S(1)}, pred[512,768]{1,0:T(8,128)(4,1)}, u32[]{:S(2)}) copy-start(pred[512,768]{1,0:T(8,128)(4,1)} %compare_or_fusion.1) | copy-start | bytes 1179652
  112.6 6.9 %collective-permute-start.1 = (bf16[128,384]{0,1:T(8,128)(2,1)S(1)}, bf16[128,384]{0,1:T(8,128)(2,1)S(1)}, u32[]{:S(2)}, u32[]{:S(2)}) collective-permute-start(bf16[128,384]{0,1:T(8,128)(2,1)S(1)} %get-tuple-element.61), channel_id=1, source_target_pairs={{4,0},{8,4},{12,8},{16,12},{20,16},{24,20},{28,24},{5,1},{9,5},{13... | collective-permute-start | bytes 294920 | tf_op jit(solution)/shard_map/ppermute | solution.py:27
  114.0 6.8 %collective-permute-start = (bf16[128,384]{0,1:T(8,128)(2,1)S(1)}, bf16[128,384]{0,1:T(8,128)(2,1)S(1)}, u32[]{:S(2)}, u32[]{:S(2)}) collective-permute-start(bf16[128,384]{0,1:T(8,128)(2,1)S(1)} %get-tuple-element.62), channel_id=1, source_target_pairs={{0,4},{4,8},{8,12},{12,16},{16,20},{20,24},{24,28},{1,5},{5,9},{9,... | collective-permute-start | bytes 294920 | tf_op jit(solution)/shard_map/ppermute | solution.py:25
  119.5 5.8 %copy-start.6 = (bf16[512,192]{0,1:T(8,128)(2,1)}, bf16[512,192]{0,1:T(8,128)(2,1)S(1)}, u32[]{:S(2)}) copy-start(bf16[512,192]{0,1:T(8,128)(2,1)S(1)} %get-tuple-element.64) | copy-start | bytes 589828
  125.3 2.7 copy-start.13
  136.5 2.7 copy-start.4
  139.2 2.3 copy-start.3
  139.3 2.3 copy-start.15
  139.8 4.6 %slice-start = ((s8[4718592]{0:T(1024)(128)(4,1)}), s8[524288]{0:T(1024)(128)(4,1)S(1)}, s32[]{:S(2)}) async-start(s8[4718592]{0:T(1024)(128)(4,1)} %bitcast.155), calls=%async_computation.3 | async-start | bytes 1048576
  141.6 1.4 copy-start.8
  141.6 2.8 slice-start.1
  143.0 1.4 copy-start.14
  144.3 19.4 %copy-start.10 = (bf16[3,64,512]{2,1,0:T(8,128)(2,1)}, bf16[3,64,512]{2,1,0:T(8,128)(2,1)S(1)}, u32[]{:S(2)}) copy-start(bf16[3,64,512]{2,1,0:T(8,128)(2,1)S(1)} %convolution_convert_fusion.2) | copy-start | bytes 589828
  144.4 1.4 copy-start.7
  147.1 9.0 %copy-start.5 = (bf16[3,64,512]{2,1,0:T(8,128)(2,1)S(1)}, bf16[3,64,512]{2,1,0:T(8,128)(2,1)}, u32[]{:S(2)}) copy-start(bf16[3,64,512]{2,1,0:T(8,128)(2,1)} %get-tuple-element.106) | copy-start | bytes 589828
  147.1 7.6 %collective-permute-start.2 = (f32[128,384]{0,1:T(8,128)S(1)}, f32[128,384]{0,1:T(8,128)S(1)}, u32[]{:S(2)}, u32[]{:S(2)}) collective-permute-start(f32[128,384]{0,1:T(8,128)S(1)} %slice.336), channel_id=1, source_target_pairs={{0,4},{4,8},{8,12},{12,16},{16,20},{20,24},{24,28},{1,5},{5,9},{9,... | collective-permute-start | bytes 589832 | tf_op jit(solution)/shard_map/ppermute | solution.py:25
  154.8 8.8 %collective-permute-start.3 = (f32[128,384]{0,1:T(8,128)S(1)}, f32[128,384]{0,1:T(8,128)S(1)}, u32[]{:S(2)}, u32[]{:S(2)}) collective-permute-start(f32[128,384]{0,1:T(8,128)S(1)} %get-tuple-element.59), channel_id=1, source_target_pairs={{4,0},{8,4},{12,8},{16,12},{20,16},{24,20},{28,24},{5,1},{9,5},{13... | collective-permute-start | bytes 589832 | tf_op jit(solution)/shard_map/ppermute | solution.py:27
  156.1 7.7 %copy-start.2 = (f32[1024,768]{0,1:T(8,128)S(1)}, f32[1024,768]{0,1:T(8,128)}, u32[]{:S(2)}) copy-start(f32[1024,768]{0,1:T(8,128)} %copy-done.1) | copy-start | bytes 9437188
  166.2 0.9 copy-start.11
  166.2 114.2 %all-gather.3.cloned.1.call-start = ((), (), s32[]{:S(2)}) async-start(), calls=%async_computation.1 | async-start | bytes 15728640 | tf_op jit(solution)/shard_map/all_gather | solution.py:12
Sparse Core Ops, SparseCore 0:
  166.4 109.2 all-reduce.3
Sparse Core Ops, SparseCore 1:
  171.5 82.6 all-gather.2
